TPU v7x, 32 devices: a whole 2x2x4 slice. The times are simulated.
32 devices in a mesh: row: 4 (over y, x), col: 8 (over z, core).
Axes of the slice: x: 2, y: 2, z: 4, core: 2. Of those that a mesh axis runs over, the one named last changes fastest.
Arguments:
- stiffness: float32 [12, 4, 128, 6144], P(None, 'row', None, 'col'), may hold values from -8 to 8
- lower_first: float32 [1024, 10, 4, 128], P('col', None, 'row'), may hold values from -0.1875 to 0.1875
- lower_second: float32 [1024, 8, 4, 128], P('col', None, 'row'), may hold values from -0.1875 to 0.1875
- diag_inv: float32 [2, 1024, 2, 4, 128], P(None, 'col', None, 'row'), as said below
Outputs:
- reduced: float32 [12, 4, 128, 6144], P(None, 'row', None, 'col')
Inputs may be any that keep to these rules, and one draw needn't show every extreme that they name: Each block of diag_inv, read as a 1024 x 1024 matrix, is zero above its diagonal and has a positive diagonal.
All inputs are finite; a program needn't handle non-finite values.
Results may differ from a plain program's by a relative error of at most 0.000086.
Values sent between devices are 32-bit elements; how exact they have to be, the bound alone decides.
A program may use at most 128 MiB of HBM per device.

v0:
```python
import jax
import jax.numpy as jnp
from jax import lax
from jax.sharding import PartitionSpec as P


def product(left, right):
    return jnp.dot(left, right, precision=lax.Precision.HIGHEST, preferred_element_type=jnp.float32)


def apply_cols(columns, factor):
    return lax.dot_general(
        columns,
        factor,
        (((0,), (0,)), ((), ())),
        precision=lax.Precision.HIGHEST,
        preferred_element_type=jnp.float32,
    )


def shards(stiffness, lower_first, lower_second, diag_inv):
    cycles = stiffness.shape[0]
    rblk = stiffness.shape[2]
    cdev = stiffness.shape[3]
    pcount = diag_inv.shape[2]
    nrow = lax.axis_size("row")
    nb = diag_inv.shape[1] * lax.axis_size("col")
    height = pcount * rblk
    matrix_rows = stiffness.reshape(cycles * rblk, cdev)
    inv_cols = lax.all_gather(diag_inv, "col", axis=1, tiled=True)
    inverse = inv_cols.reshape(2, nb, height)

    def own_rows(solved):
        grouped = solved.reshape(pcount, nrow, rblk, cdev)
        mine = lax.dynamic_slice_in_dim(grouped, lax.axis_index("row"), 1, 1)
        return mine.reshape(height, cdev)

    w_first = lax.psum(product(inverse[0], matrix_rows[:height]), "row")
    coupling = lax.all_gather(lower_first[:, :pcount], "col", axis=0, tiled=True).reshape(
        nb, height
    )
    w_second = lax.psum(
        product(inverse[1], matrix_rows[height : 2 * height] - apply_cols(coupling, w_first)), "row"
    )
    pieces = (
        lax.all_gather(lower_first[:, pcount:], "col", axis=0, tiled=True),
        lax.all_gather(lower_second, "col", axis=0, tiled=True),
    )
    count = pieces[0].shape[0]
    first_piece = pieces[0].reshape(count, -1)
    second_piece = pieces[1].reshape(count, -1)
    remain = (
        matrix_rows[2 * height :]
        - apply_cols(first_piece, w_first)
        - apply_cols(second_piece, w_second)
    )
    stacked = jnp.concatenate([own_rows(w_first), own_rows(w_second), remain], axis=0)
    return stacked.reshape(cycles, 1, rblk, cdev)


def solution(mesh):
    placed = (
        P(None, "row", None, "col"),
        P("col", None, "row", None),
        P("col", None, "row", None),
        P(None, "col", None, "row", None),
    )
    return jax.shard_map(
        shards, mesh=mesh, in_specs=placed, out_specs=P(None, "row", None, "col"), check_vma=False
    )
```

profile of v0, /device:TPU:0, one launch (start us, length us, event | category | flops | bytes accessed | tf_op | source)
XLA Modules:
  0.0 378.0 jit_solution(10535140194078627687)
XLA Ops:
  7.3 1.6 slice.37
  8.9 1.5 fusion.16
  10.4 30.4 %all-gather.5.cloned.1.call-done = f32[2,1024,2,1,128]{4,3,2,1,0:T(1,128)} async-done(((f32[2,128,2,1,128]{4,3,2,1,0:T(1,128)}), f32[2,1024,2,1,128]{4,3,2,1,0:T(1,128)}) %all-gather.5.cloned.1.call-update) | async-done | bytes 2097168 | tf_op jit(solution)/shard_map/all_gather | solution.py:30
  40.8 7.8 %slice_reduce_fusion = (f32[1024,2,128]{2,1,0:T(2,128)S(1)}, f32[1024,2,128]{2,1,0:T(2,128)S(1)}) fusion(f32[2,1024,2,1,128]{4,3,2,1,0:T(1,128)} %all-gather.5.cloned.1.call-done), kind=kLoop, calls=%fused_computation.19 | loop fusion | bytes 4194304 | tf_op jit(solution)/shard_map/slice | solution.py:43
  48.7 4.4 %fusion.13 = f32[1024,768]{1,0:T(8,128)} fusion(f32[256,768]{1,0:T(8,128)S(1)} %bitcast.71, f32[128,8,2,128]{3,2,1,0:T(2,128)S(1)} %bitcast.68), kind=kOutput, calls=%fused_computation.16 | convolution fusion | flops 2415919104 | bytes 4980736 | tf_op jit(solution)/shard_map/dot_general | solution.py:8
  53.6 10.5 %all-gather.7.cloned.1.call-done = f32[1024,2,1,128]{3,1,2,0:T(2,128)} async-done(((f32[128,2,1,128]{3,1,2,0:T(2,128)}), f32[1024,2,1,128]{3,1,2,0:T(2,128)}) %all-gather.7.cloned.1.call-update) | async-done | bytes 1048592 | tf_op jit(solution)/shard_map/all_gather | solution.py:39
  64.1 89.7 %all-reduce.3.cloned.1.call-done = f32[1024,768]{1,0:T(8,128)} async-done(((f32[1024,768]{1,0:T(8,128)}), f32[1024,768]{1,0:T(8,128)}) %all-reduce.3.cloned.1.call-update) | async-done | bytes 3145744 | tf_op jit(solution)/shard_map/psum | solution.py:38
  153.8 7.2 %fusion.8 = f32[256,768]{0,1:T(8,128)S(1)} fusion(f32[256,768]{0,1:T(8,128)S(1)} %copy.21, f32[1024,768]{1,0:T(8,128)} %all-reduce.3.cloned.1.call-done, f32[128,8,2,128]{3,2,1,0:T(2,128)} %bitcast.76), kind=kOutput, calls=%fused_computation.11 | convolution fusion | flops 2416115712 | bytes 5767168 | tf_op jit(solution)/shard_map/dot_general | solution.py:12
  161.0 4.4 %convolution_bitcast_fusion = f32[1024,768]{0,1:T(8,128)} fusion(f32[256,768]{0,1:T(8,128)S(1)} %fusion.8, f32[128,8,2,128]{3,2,1,0:T(2,128)S(1)} %bitcast.67), kind=kOutput, calls=%fused_computation.9 | convolution fusion | flops 2415919104 | bytes 4980736 | tf_op jit(solution)/shard_map/dot_general | solution.py:8
  166.3 0.8 slice.41
  167.2 3.8 slice.39
  170.9 4.1 %copy.22 = f32[1024,768]{0,1:T(8,128)} copy(f32[1024,768]{1,0:T(8,128)} %bitcast.65) | data formatting | bytes 6291456 | tf_op jit(solution)/shard_map/slice | solution.py:53
  175.1 0.9 constant_dynamic-slice_fusion
  176.0 2.3 copy.20
  178.3 74.2 %all-reduce.5.cloned.1.call-done = f32[1024,768]{0,1:T(8,128)} async-done(((f32[1024,768]{0,1:T(8,128)}), f32[1024,768]{0,1:T(8,128)}) %all-reduce.5.cloned.1.call-update) | async-done | bytes 3145744 | tf_op jit(solution)/shard_map/psum | solution.py:42
  252.5 5.1 %reshape.36 = f32[2,4,128,768]{2,1,0,3:T(4,128)} reshape(f32[1024,768]{0,1:T(8,128)} %all-reduce.5.cloned.1.call-done) | data formatting | bytes 6291456 | tf_op jit(solution)/shard_map/reshape | solution.py:34
  257.7 4.6 %dynamic-slice_reduce_fusion = f32[2,128,768]{1,0,2:T(2,128)S(1)} fusion(f32[2,4,128,768]{2,1,0,3:T(4,128)} %reshape.36, s32[]{:T(128)S(6)} %select_n.4), kind=kLoop, calls=%fused_computation.22 | loop fusion | bytes 1572868 | tf_op jit(solution)/shard_map/dynamic_slice | solution.py:35
  262.2 0.9 copy.54
  263.2 37.7 %all-gather.11.cloned.1.call-done = f32[1024,8,1,128]{3,1,2,0:T(8,128)} async-done(((f32[128,8,1,128]{3,1,2,0:T(8,128)}), f32[1024,8,1,128]{3,1,2,0:T(8,128)}) %all-gather.11.cloned.1.call-update) | async-done | bytes 4194320 | tf_op jit(solution)/shard_map/all_gather | solution.py:47
  300.9 14.8 %fusion = f32[768,1024]{1,0:T(8,128)} fusion(f32[1024,768]{0,1:T(8,128)} %all-reduce.5.cloned.1.call-done, f32[128,8,8,128]{3,2,1,0:T(8,128)} %bitcast.66), kind=kOutput, calls=%fused_computation.1 | convolution fusion | flops 9663676416 | bytes 10485760 | tf_op jit(solution)/shard_map/dot_general | solution.py:12
  315.6 32.4 %all-gather.9.cloned.1.call-done = f32[1024,8,1,128]{3,1,2,0:T(8,128)} async-done(((f32[128,8,1,128]{3,1,2,0:T(8,128)}), f32[1024,8,1,128]{3,1,2,0:T(8,128)}) %all-gather.9.cloned.1.call-update) | async-done | bytes 4194320 | tf_op jit(solution)/shard_map/all_gather | solution.py:46
  348.0 14.4 %bitcast_subtract_fusion = f32[1024,768]{0,1:T(8,128)S(1)} fusion(f32[768,1024]{1,0:T(8,128)} %fusion, f32[1024,768]{0,1:T(8,128)} %copy.22, f32[1024,768]{1,0:T(8,128)S(1)} %copy-done, f32[128,8,8,128]{3,2,1,0:T(8,128)} %bitcast.69), kind=kOutput, calls=%fused_computation.7 | convolution fusion | flops 9665249280 | bytes 16777216 | tf_op jit(solution)/shard_map/dot_general | solution.py:12
  362.5 2.6 pad_maximum_fusion
  365.1 6.0 %copy.18 = f32[1536,768]{1,0:T(8,128)} copy(f32[1536,768]{0,1:T(8,128)} %pad_maximum_fusion) | data formatting | bytes 9437184 | tf_op jit(solution)/shard_map/concatenate | solution.py:57
  (21 shorter events, 2.2 us)
Async XLA Ops:
  6.5 34.3 %all-gather.5.cloned.1.call-start = ((), (), s32[]{:S(2)}) async-start(), calls=%async_computation | async-start | bytes 2359296 | tf_op jit(solution)/shard_map/all_gather | solution.py:30
  7.3 56.9 %all-gather.7.cloned.1.call-start = ((), (), s32[]{:S(2)}) async-start(), calls=%async_computation.2 | async-start | bytes 1179648 | tf_op jit(solution)/shard_map/all_gather | solution.py:39
  8.9 144.9 %all-reduce.3.cloned.1.call-start = ((), (), s32[]{:S(2)}) async-start(), calls=%async_computation.1 | async-start | bytes 6291456 | tf_op jit(solution)/shard_map/psum | solution.py:38
  53.1 199.4 %all-reduce.5.cloned.1.call-start = ((), (), s32[]{:S(2)}) async-start(), calls=%async_computation.3 | async-start | bytes 6291456 | tf_op jit(solution)/shard_map/psum | solution.py:42
  161.0 5.3 %copy-start.3 = (f32[128,10,1,128]{3,2,1,0:T(1,128)S(1)}, f32[128,10,1,128]{3,2,1,0:T(1,128)}, u32[]{:S(2)}) copy-start(f32[128,10,1,128]{3,2,1,0:T(1,128)} %param.5) | copy-start | bytes 1966084
  165.4 135.4 %all-gather.11.cloned.1.call-start = ((), (), s32[]{:S(2)}) async-start(), calls=%async_computation.5 | async-start | bytes 4718592 | tf_op jit(solution)/shard_map/all_gather | solution.py:47
  166.0 182.0 %all-gather.9.cloned.1.call-start = ((), (), s32[]{:S(2)}) async-start(), calls=%async_computation.4 | async-start | bytes 4718592 | tf_op jit(solution)/shard_map/all_gather | solution.py:46
  170.9 4.1 %copy-start = (f32[1024,768]{1,0:T(8,128)S(1)}, f32[1024,768]{1,0:T(8,128)}, u32[]{:S(2)}) copy-start(f32[1024,768]{1,0:T(8,128)} %all-reduce.3.cloned.1.call-done) | copy-start | bytes 9437188
  348.0 14.4 %copy-start.1 = (f32[256,768]{0,1:T(8,128)S(1)}, f32[256,768]{0,1:T(8,128)}, u32[]{:S(2)}) copy-start(f32[256,768]{0,1:T(8,128)} %copy.20) | copy-start | bytes 2359300
  348.0 14.4 %copy-start.2 = (f32[96,8,2,128]{3,1,2,0:T(8,128)S(1)}, f32[96,8,2,128]{3,1,2,0:T(8,128)}, u32[]{:S(2)}) copy-start(f32[96,8,2,128]{3,1,2,0:T(8,128)} %copy.54) | copy-start | bytes 2359300
Sparse Core Ops, SparseCore 0:
  8.9 31.8 all-gather.4
  42.4 21.6 all-gather.6
  67.2 86.5 all-reduce.2
  165.5 86.9 all-reduce.4
  254.0 46.8 all-gather.10
  302.3 45.6 all-gather.8
where the time goes:
time: 378 us
  waiting for transfers between devices  276 us (73%)
  matrix products  45.1 us (12%)
  local copies, waits for them, and re-layouts  39.8 us (11%)
  between operations  13.6 us (4%)
    psum x1, waiting for transfers between devices, shards(): w_first = lax.psum(product(inverse[0], matrix_rows[:height]), 'row')  89.7 us
    psum x1, waiting for transfers between devices, shards(): lax.psum(product(inverse[1], matrix_rows[height:2 * height] - apply_cols(...  74.2 us
    all_gather x1, waiting for transfers between devices, shards(): lax.all_gather(lower_second, 'col', axis=0, tiled=True)  37.7 us
    dot_general x3, matrix products, apply_cols(): lax.dot_general(columns, factor, (((0,), (0,)), ((), ())), precision=lax....  36.4 us
    all_gather x1, waiting for transfers between devices, shards(): lax.all_gather(lower_first[:, pcount:], 'col', axis=0, tiled=True)  32.4 us
    all_gather x1, waiting for transfers between devices, shards(): inv_cols = lax.all_gather(diag_inv, 'col', axis=1, tiled=True)  30.4 us
    all_gather x1, waiting for transfers between devices, shards(): lax.all_gather(lower_first[:, :pcount], 'col', axis=0, tiled=True)  10.5 us
    dot_general x2, matrix products, product(): jnp.dot(left, right, precision=lax.Precision.HIGHEST, preferred_element_t...  8.73 us
  transfers between devices with their start and end apart: 6, of which 6 were waited for; matrix products, arithmetic and copies ran while one was open for 14% of the time, Pallas kernels for 0%

commit v1 on v0

--- a/solution.py
+++ b/solution.py
@@ -27,7 +27,12 @@
     nb = diag_inv.shape[1] * lax.axis_size("col")
     height = pcount * rblk
     matrix_rows = stiffness.reshape(cycles * rblk, cdev)
-    inv_cols = lax.all_gather(diag_inv, "col", axis=1, tiled=True)
+    ring = [diag_inv]
+    for hop in range(7):
+        ring.append(lax.ppermute(ring[-1], "col", [(dev, (dev + 1) % 8) for dev in range(8)]))
+    inv_cols = jnp.roll(
+        jnp.concatenate(ring[::-1], axis=1), (lax.axis_index("col") + 1) * ring[0].shape[1], axis=1
+    )
     inverse = inv_cols.reshape(2, nb, height)
 
     def own_rows(solved):

time: 378 us -> 311 us (0.82)
  waiting for transfers between devices: 276 us -> 211 us
  local copies, waits for them, and re-layouts: 39.8 us -> 35.6 us
    ppermute x0 -> x7, waiting for transfers between devices: none -> 50.9 us  [shards(): lax.ppermute(ring[-1], 'col', [(dev, (dev + 1) % 8) for dev in range(8)])]
    all_gather x1, waiting for transfers between devices: 37.7 us -> 0.01 us  [shards(): lax.all_gather(lower_second, 'col', axis=0, tiled=True)]
    all_gather x1, waiting for transfers between devices: 32.4 us -> 0.01 us  [shards(): lax.all_gather(lower_first[:, pcount:], 'col', axis=0, tiled=True)]
    all_gather x1 -> x0, waiting for transfers between devices: 30.4 us -> none  [shards(): inv_cols = lax.all_gather(diag_inv, 'col', axis=1, tiled=True)]
    all_gather x1, waiting for transfers between devices: 10.5 us -> 0.02 us  [shards(): lax.all_gather(lower_first[:, :pcount], 'col', axis=0, tiled=True)]
    reshape x1 -> x0, local copies, waits for them, and re-layouts: 5.13 us -> none  [own_rows(): grouped = solved.reshape(pcount, nrow, rblk, cdev)]
    psum x1, waiting for transfers between devices: 89.7 us -> 85.5 us  [shards(): w_first = lax.psum(product(inverse[0], matrix_rows[:height]), 'row')]
  transfers between devices with their start and end apart: 6 -> 12, of which waited for: 6 -> 9; matrix products, arithmetic and copies ran while one was open for 14% -> 16% of each run, Pallas kernels for 0% -> 0%
where the time goes in v1:
time: 311 us; the launch traced here: 310 us
  waiting for transfers between devices  211 us (68%)
  matrix products  45.5 us (15%)
  local copies, waits for them, and re-layouts  35.6 us (11%)
  between operations  14.8 us (5%)
    psum x1, waiting for transfers between devices, shards(): w_first = lax.psum(product(inverse[0], matrix_rows[:height]), 'row')  85.5 us
    psum x1, waiting for transfers between devices, shards(): lax.psum(product(inverse[1], matrix_rows[height:2 * height] - apply_cols(...  73.6 us
    ppermute x7, waiting for transfers between devices, shards(): lax.ppermute(ring[-1], 'col', [(dev, (dev + 1) % 8) for dev in range(8)])  50.9 us
    dot_general x3, matrix products, apply_cols(): lax.dot_general(columns, factor, (((0,), (0,)), ((), ())), precision=lax....  36.6 us
    dot_general x2, matrix products, product(): jnp.dot(left, right, precision=lax.Precision.HIGHEST, preferred_element_t...  8.94 us
    slice x2, local copies, waits for them, and re-layouts, shards(): matrix_rows[2 * height:] - apply_cols(first_piece, w_first)  7.9 us
    slice x1, local copies, waits for them, and re-layouts, shards(): inverse[1]  6.61 us
  transfers between devices with their start and end apart: 12, of which 9 were waited for; matrix products, arithmetic and copies ran while one was open for 16% of the time, Pallas kernels for 0%

profile of v1, /device:TPU:0, one launch (start us, length us, event | category | flops | bytes accessed | tf_op | source)
XLA Modules:
  0.0 310.3 jit_solution(14289034947705757908)
XLA Ops:
  7.9 8.4 %collective-permute-done = f32[2,128,2,1,128]{4,3,2,1,0:T(1,128)S(1)} collective-permute-done((f32[2,128,2,1,128]{4,3,2,1,0:T(1,128)}, f32[2,128,2,1,128]{4,3,2,1,0:T(1,128)S(1)}, u32[]{:S(2)}, u32[]{:S(2)}) %collective-permute-start) | collective-permute-done | bytes 262176 | tf_op jit(solution)/shard_map/ppermute | solution.py:32
  16.2 7.6 %collective-permute-done.1 = f32[2,128,2,1,128]{4,3,2,1,0:T(1,128)S(1)} collective-permute-done((f32[2,128,2,1,128]{4,3,2,1,0:T(1,128)S(1)}, f32[2,128,2,1,128]{4,3,2,1,0:T(1,128)S(1)}, u32[]{:S(2)}, u32[]{:S(2)}) %collective-permute-start.1) | collective-permute-done | bytes 262176 | tf_op jit(solution)/shard_map/ppermute | solution.py:32
  23.8 7.6 %collective-permute-done.2 = f32[2,128,2,1,128]{4,3,2,1,0:T(1,128)S(1)} collective-permute-done((f32[2,128,2,1,128]{4,3,2,1,0:T(1,128)S(1)}, f32[2,128,2,1,128]{4,3,2,1,0:T(1,128)S(1)}, u32[]{:S(2)}, u32[]{:S(2)}) %collective-permute-start.2) | collective-permute-done | bytes 262176 | tf_op jit(solution)/shard_map/ppermute | solution.py:32
  31.4 7.6 %collective-permute-done.3 = f32[2,128,2,1,128]{4,3,2,1,0:T(1,128)S(1)} collective-permute-done((f32[2,128,2,1,128]{4,3,2,1,0:T(1,128)S(1)}, f32[2,128,2,1,128]{4,3,2,1,0:T(1,128)S(1)}, u32[]{:S(2)}, u32[]{:S(2)}) %collective-permute-start.3) | collective-permute-done | bytes 262176 | tf_op jit(solution)/shard_map/ppermute | solution.py:32
  39.0 7.6 %collective-permute-done.4 = f32[2,128,2,1,128]{4,3,2,1,0:T(1,128)S(1)} collective-permute-done((f32[2,128,2,1,128]{4,3,2,1,0:T(1,128)S(1)}, f32[2,128,2,1,128]{4,3,2,1,0:T(1,128)S(1)}, u32[]{:S(2)}, u32[]{:S(2)}) %collective-permute-start.4) | collective-permute-done | bytes 262176 | tf_op jit(solution)/shard_map/ppermute | solution.py:32
  46.6 1.6 slice.38
  48.3 5.9 %collective-permute-done.5 = f32[2,128,2,1,128]{4,3,2,1,0:T(1,128)S(1)} collective-permute-done((f32[2,128,2,1,128]{4,3,2,1,0:T(1,128)S(1)}, f32[2,128,2,1,128]{4,3,2,1,0:T(1,128)S(1)}, u32[]{:S(2)}, u32[]{:S(2)}) %collective-permute-start.5) | collective-permute-done | bytes 262176 | tf_op jit(solution)/shard_map/ppermute | solution.py:32
  54.2 1.5 fusion.17
  55.7 6.3 %collective-permute-done.6 = f32[2,128,2,1,128]{4,3,2,1,0:T(1,128)S(1)} collective-permute-done((f32[2,128,2,1,128]{4,3,2,1,0:T(1,128)S(1)}, f32[2,128,2,1,128]{4,3,2,1,0:T(1,128)S(1)}, u32[]{:S(2)}, u32[]{:S(2)}) %collective-permute-start.6) | collective-permute-done | bytes 262176 | tf_op jit(solution)/shard_map/ppermute | solution.py:32
  65.3 6.6 %dynamic-slice_reduce_fusion = (f32[1024,2,128]{2,1,0:T(2,128)S(1)}, f32[1024,2,128]{2,1,0:T(2,128)S(1)}) fusion(f32[2,2048,2,1,128]{4,3,2,1,0:T(1,128)S(1)} %constant_dynamic-update-slice_fusion, s32[]{:T(128)S(6)} %add.29, s32[]{:T(128)S(6)} %select_n.18), kind=kLoop, calls=%fused_computation.19 | loop fusion | bytes 4194312 | tf_op jit(solution)/shard_map/slice | solution.py:48
  71.9 4.6 %fusion.14 = f32[1024,768]{1,0:T(8,128)} fusion(f32[256,768]{1,0:T(8,128)S(1)} %bitcast.61, f32[128,8,2,128]{3,2,1,0:T(2,128)S(1)} %bitcast.59), kind=kOutput, calls=%fused_computation.16 | convolution fusion | flops 2415919104 | bytes 4980736 | tf_op jit(solution)/shard_map/dot_general | solution.py:8
  76.8 85.5 %all-reduce.3.cloned.1.call-done = f32[1024,768]{1,0:T(8,128)} async-done(((f32[1024,768]{1,0:T(8,128)}), f32[1024,768]{1,0:T(8,128)}) %all-reduce.3.cloned.1.call-update) | async-done | bytes 3145744 | tf_op jit(solution)/shard_map/psum | solution.py:43
  162.3 7.2 %fusion.8 = f32[256,768]{0,1:T(8,128)S(1)} fusion(f32[256,768]{0,1:T(8,128)S(1)} %copy.24, f32[1024,768]{1,0:T(8,128)} %all-reduce.3.cloned.1.call-done, f32[128,8,2,128]{3,2,1,0:T(2,128)} %bitcast.66), kind=kOutput, calls=%fused_computation.10 | convolution fusion | flops 2416115712 | bytes 5767168 | tf_op jit(solution)/shard_map/dot_general | solution.py:12
  169.6 4.4 %fusion.11 = f32[1024,768]{1,0:T(8,128)} fusion(f32[256,768]{0,1:T(8,128)S(1)} %fusion.8, f32[128,8,2,128]{3,2,1,0:T(2,128)S(1)} %bitcast.58), kind=kOutput, calls=%fused_computation.13 | convolution fusion | flops 2415919104 | bytes 4980736 | tf_op jit(solution)/shard_map/dot_general | solution.py:8
  175.8 3.8 %slice.39 = f32[8,1,128,768]{3,2,1,0:T(8,128)} slice(f32[12,1,128,768]{3,2,1,0:T(8,128)} %param.4), slice={[4:12], [0:1], [0:128], [0:768]} | slice | bytes 6291456 | tf_op jit(solution)/shard_map/slice | solution.py:58
  179.6 4.1 %copy.26 = f32[1024,768]{0,1:T(8,128)} copy(f32[1024,768]{1,0:T(8,128)} %bitcast.57) | data formatting | bytes 6291456 | tf_op jit(solution)/shard_map/slice | solution.py:58
  184.7 2.4 copy.23
  187.1 73.6 %all-reduce.5.cloned.1.call-done = f32[1024,768]{1,0:T(8,128)} async-done(((f32[1024,768]{1,0:T(8,128)}), f32[1024,768]{1,0:T(8,128)}) %all-reduce.5.cloned.1.call-update) | async-done | bytes 3145744 | tf_op jit(solution)/shard_map/psum | solution.py:47
  260.7 2.1 constant_dynamic-slice_fusion
  262.8 2.3 copy.25
  265.1 14.7 %fusion = f32[768,1024]{1,0:T(8,128)} fusion(f32[1024,768]{1,0:T(8,128)} %all-reduce.5.cloned.1.call-done, f32[128,8,8,128]{3,2,1,0:T(8,128)} %bitcast.70), kind=kOutput, calls=%fused_computation.1 | convolution fusion | flops 9663676416 | bytes 10485760 | tf_op jit(solution)/shard_map/dot_general | solution.py:12
  279.8 14.7 %bitcast_subtract_fusion = f32[1024,768]{0,1:T(8,128)S(1)} fusion(f32[768,1024]{1,0:T(8,128)} %fusion, f32[1024,768]{0,1:T(8,128)} %copy.26, f32[1024,768]{1,0:T(8,128)S(1)} %copy-done, f32[128,8,8,128]{3,2,1,0:T(8,128)} %bitcast.60), kind=kOutput, calls=%fused_computation.7 | convolution fusion | flops 9665249280 | bytes 16777216 | tf_op jit(solution)/shard_map/dot_general | solution.py:12
  294.5 2.6 pad_maximum_fusion
  297.1 6.0 %copy.21 = f32[1536,768]{1,0:T(8,128)} copy(f32[1536,768]{0,1:T(8,128)} %pad_maximum_fusion) | data formatting | bytes 9437184 | tf_op jit(solution)/shard_map/concatenate | solution.py:62
  (49 shorter events, 6.9 us)
Async XLA Ops:
  7.4 56.0 %copy-start.3 = (f32[2,128,2,1,128]{4,3,2,1,0:T(1,128)S(1)}, f32[2,128,2,1,128]{4,3,2,1,0:T(1,128)}, u32[]{:S(2)}) copy-start(f32[2,128,2,1,128]{4,3,2,1,0:T(1,128)} %param.7) | copy-start | bytes 786436
  7.4 69.4 %all-gather.4.cloned.1.call-start = ((), (), s32[]{:S(2)}) async-start(), calls=%async_computation.1 | async-start | bytes 1179648 | tf_op jit(solution)/shard_map/all_gather | solution.py:44
  7.4 8.8 %collective-permute-start = (f32[2,128,2,1,128]{4,3,2,1,0:T(1,128)}, f32[2,128,2,1,128]{4,3,2,1,0:T(1,128)S(1)}, u32[]{:S(2)}, u32[]{:S(2)}) collective-permute-start(f32[2,128,2,1,128]{4,3,2,1,0:T(1,128)} %param.7), channel_id=1, source_target_pairs={{0,1},{1,2},{2,3},{3,4},{4,5},{5,6},{6,7},{7,0},{8,9},{9,10},{10,1... | collective-permute-start | bytes 786440 | tf_op jit(solution)/shard_map/ppermute | solution.py:32
  16.2 7.6 %collective-permute-start.1 = (f32[2,128,2,1,128]{4,3,2,1,0:T(1,128)S(1)}, f32[2,128,2,1,128]{4,3,2,1,0:T(1,128)S(1)}, u32[]{:S(2)}, u32[]{:S(2)}) collective-permute-start(f32[2,128,2,1,128]{4,3,2,1,0:T(1,128)S(1)} %collective-permute-done), channel_id=1, source_target_pairs={{0,1},{1,2},{2,3},{3,4},{4,5},{5,6},{6,7},{7,0},{8,9},{9,10},{10,1... | collective-permute-start | bytes 786440 | tf_op jit(solution)/shard_map/ppermute | solution.py:32
  23.8 7.6 %collective-permute-start.2 = (f32[2,128,2,1,128]{4,3,2,1,0:T(1,128)S(1)}, f32[2,128,2,1,128]{4,3,2,1,0:T(1,128)S(1)}, u32[]{:S(2)}, u32[]{:S(2)}) collective-permute-start(f32[2,128,2,1,128]{4,3,2,1,0:T(1,128)S(1)} %collective-permute-done.1), channel_id=1, source_target_pairs={{0,1},{1,2},{2,3},{3,4},{4,5},{5,6},{6,7},{7,0},{8,9},{9,10},{10,1... | collective-permute-start | bytes 786440 | tf_op jit(solution)/shard_map/ppermute | solution.py:32
  31.4 7.6 %collective-permute-start.3 = (f32[2,128,2,1,128]{4,3,2,1,0:T(1,128)S(1)}, f32[2,128,2,1,128]{4,3,2,1,0:T(1,128)S(1)}, u32[]{:S(2)}, u32[]{:S(2)}) collective-permute-start(f32[2,128,2,1,128]{4,3,2,1,0:T(1,128)S(1)} %collective-permute-done.2), channel_id=1, source_target_pairs={{0,1},{1,2},{2,3},{3,4},{4,5},{5,6},{6,7},{7,0},{8,9},{9,10},{10,1... | collective-permute-start | bytes 786440 | tf_op jit(solution)/shard_map/ppermute | solution.py:32
  39.0 7.6 %collective-permute-start.4 = (f32[2,128,2,1,128]{4,3,2,1,0:T(1,128)S(1)}, f32[2,128,2,1,128]{4,3,2,1,0:T(1,128)S(1)}, u32[]{:S(2)}, u32[]{:S(2)}) collective-permute-start(f32[2,128,2,1,128]{4,3,2,1,0:T(1,128)S(1)} %collective-permute-done.3), channel_id=1, source_target_pairs={{0,1},{1,2},{2,3},{3,4},{4,5},{5,6},{6,7},{7,0},{8,9},{9,10},{10,1... | collective-permute-start | bytes 786440 | tf_op jit(solution)/shard_map/ppermute | solution.py:32
  46.6 7.6 %collective-permute-start.5 = (f32[2,128,2,1,128]{4,3,2,1,0:T(1,128)S(1)}, f32[2,128,2,1,128]{4,3,2,1,0:T(1,128)S(1)}, u32[]{:S(2)}, u32[]{:S(2)}) collective-permute-start(f32[2,128,2,1,128]{4,3,2,1,0:T(1,128)S(1)} %collective-permute-done.4), channel_id=1, source_target_pairs={{0,1},{1,2},{2,3},{3,4},{4,5},{5,6},{6,7},{7,0},{8,9},{9,10},{10,1... | collective-permute-start | bytes 786440 | tf_op jit(solution)/shard_map/ppermute | solution.py:32
  48.2 114.1 %all-reduce.3.cloned.1.call-start = ((), (), s32[]{:S(2)}) async-start(), calls=%async_computation | async-start | bytes 6291456 | tf_op jit(solution)/shard_map/psum | solution.py:43
  54.2 7.8 %collective-permute-start.6 = (f32[2,128,2,1,128]{4,3,2,1,0:T(1,128)S(1)}, f32[2,128,2,1,128]{4,3,2,1,0:T(1,128)S(1)}, u32[]{:S(2)}, u32[]{:S(2)}) collective-permute-start(f32[2,128,2,1,128]{4,3,2,1,0:T(1,128)S(1)} %collective-permute-done.5), channel_id=1, source_target_pairs={{0,1},{1,2},{2,3},{3,4},{4,5},{5,6},{6,7},{7,0},{8,9},{9,10},{10,1... | collective-permute-start | bytes 786440 | tf_op jit(solution)/shard_map/ppermute | solution.py:32
  76.5 184.3 %all-reduce.5.cloned.1.call-start = ((), (), s32[]{:S(2)}) async-start(), calls=%async_computation.2 | async-start | bytes 6291456 | tf_op jit(solution)/shard_map/psum | solution.py:47
  169.6 5.4 %copy-start.4 = (f32[128,10,1,128]{3,2,1,0:T(1,128)S(1)}, f32[128,10,1,128]{3,2,1,0:T(1,128)}, u32[]{:S(2)}) copy-start(f32[128,10,1,128]{3,2,1,0:T(1,128)} %param.5) | copy-start | bytes 1966084
  174.0 91.1 %all-gather.8.cloned.1.call-start = ((), (), s32[]{:S(2)}) async-start(), calls=%async_computation.4 | async-start | bytes 4718592 | tf_op jit(solution)/shard_map/all_gather | solution.py:52
  174.7 105.0 %all-gather.6.cloned.1.call-start = ((), (), s32[]{:S(2)}) async-start(), calls=%async_computation.3 | async-start | bytes 4718592 | tf_op jit(solution)/shard_map/all_gather | solution.py:51
  179.6 4.1 %copy-start = (f32[1024,768]{1,0:T(8,128)S(1)}, f32[1024,768]{1,0:T(8,128)}, u32[]{:S(2)}) copy-start(f32[1024,768]{1,0:T(8,128)} %all-reduce.3.cloned.1.call-done) | copy-start | bytes 9437188
  279.8 14.7 %copy-start.1 = (f32[256,768]{0,1:T(8,128)S(1)}, f32[256,768]{0,1:T(8,128)}, u32[]{:S(2)}) copy-start(f32[256,768]{0,1:T(8,128)} %copy.23) | copy-start | bytes 2359300
  279.8 14.7 %copy-start.2 = (f32[256,768]{0,1:T(8,128)S(1)}, f32[256,768]{0,1:T(8,128)}, u32[]{:S(2)}) copy-start(f32[256,768]{0,1:T(8,128)} %copy.25) | copy-start | bytes 2359300
Sparse Core Ops, SparseCore 0:
  48.3 24.7 all-gather.3
  176.4 46.8 all-gather.7
  224.9 45.6 all-gather.5
Sparse Core Ops, SparseCore 1:
  76.6 85.7 all-reduce.2
  174.0 86.6 all-reduce.4
